TPU v7x, 32 devices: a whole 2x2x4 slice. The times are simulated.
32 devices in a mesh: fsdp: 8 (over y, x, core), tp: 4 (over z).
Axes of the slice: x: 2, y: 2, z: 4, core: 2. Of those that a mesh axis runs over, the one named last changes fastest.
Arguments:
- residual: bfloat16 [4096, 2048], P(('fsdp', 'tp')), may hold values from -6 to 6
- norm_gain: bfloat16 [2048], P(('fsdp', 'tp')), may hold values from 0.099609375 to 1.8984375
- norm_shift: bfloat16 [2048], P(('fsdp', 'tp')), may hold values from -1.75 to 1.75
- qkv_weight: bfloat16 [3, 2048, 2048], P(None, 'fsdp', 'tp'), may hold values from -0.125 to 0.125
- qkv_bias: bfloat16 [3, 2048], P(None, ('tp', 'fsdp')), may hold values from -1.75 to 1.75
- dense_weight: bfloat16 [2048, 2048], P('tp', 'fsdp'), may hold values from -0.75 to 0.75
- dense_bias: bfloat16 [2048], P(('fsdp', 'tp')), may hold values from -1.75 to 1.75
- inner_weight: bfloat16 [2048, 8192], P('fsdp', 'tp'), may hold values from -0.125 to 0.125
- inner_bias: bfloat16 [8192], P(('tp', 'fsdp')), may hold values from -1.75 to 1.75
- outer_weight: bfloat16 [8192, 2048], P('tp', 'fsdp'), may hold values from -0.0625 to 0.0625
- outer_bias: bfloat16 [2048], P(('fsdp', 'tp')), may hold values from -1.75 to 1.75
- cotangent: bfloat16 [4096, 2048], P(('fsdp', 'tp')), may hold values from -6 to 6
- segment: int32 [4096], replicated, may hold values from 0 to 38, as said below
- ancestors: int32 [39, 3], replicated, may hold values from 0 to 38, as said below
- valid_slot: int32 [4096], replicated, may hold values from 0 to 1, as said below
Outputs:
- output: bfloat16 [4096, 2048], P(('fsdp', 'tp'))
- residual_grad: bfloat16 [4096, 2048], P(('fsdp', 'tp'))
- norm_gain_grad: float32 [2048], P(('fsdp', 'tp'))
- norm_shift_grad: float32 [2048], P(('fsdp', 'tp'))
- qkv_weight_grad: float32 [3, 2048, 2048], P(None, 'fsdp', 'tp')
- qkv_bias_grad: float32 [3, 2048], P(None, ('tp', 'fsdp'))
- dense_weight_grad: float32 [2048, 2048], P('tp', 'fsdp')
- dense_bias_grad: float32 [2048], P(('fsdp', 'tp'))
- inner_weight_grad: float32 [2048, 8192], P('fsdp', 'tp')
- inner_bias_grad: float32 [8192], P(('tp', 'fsdp'))
- outer_weight_grad: float32 [8192, 2048], P('tp', 'fsdp')
- outer_bias_grad: float32 [2048], P(('fsdp', 'tp'))
Inputs may be any that keep to these rules, and one draw needn't show every extreme that they name: Each of the 3 trees fills 1024 consecutive slots, in order of slots: a trunk of 640 slots, then four branches and eight leaves of 32 slots each, two leaves to a branch, each leaf after its branch; the slots of a segment are consecutive and carry its id; padding slots carry 0. `ancestors`: row s names the trunk, branch and leaf segment of the path that ends in segment s, repeating s where the path is shorter; each tree's segments name only that tree's segments. `valid_slot`: 1 on exactly the slots that trees fill, 0 on the other 1024 slots.
All inputs are finite; a program needn't handle non-finite values.
Results may differ from a plain program's by a relative error of at most 0.0098.
Values may be sent and summed in bfloat16 or wider, within the bound.
No kernel may reach another device: no remote copies, remote signals or barrier semaphores. Data moves between devices by JAX's collectives and lax.ppermute only.
A program may use at most 192 MiB of HBM per device.

v0:
```python
import jax
import jax.numpy as jnp
from jax import lax
from jax.sharding import PartitionSpec as P

HEAD_DIM = 64
ROTARY = 32
TREE_LEN = 1024
EPSILON = 1e-05


def passed_along(value, axis, steps):
    count = lax.axis_size(axis)
    initial, last = (max(0, -steps), min(count, count - steps))
    return lax.ppermute(value, axis, [(source, source + steps) for source in range(initial, last)])


def norm_rows(inputs_f, gain_f, shift_f):
    row_mean = jnp.mean(inputs_f, axis=-1, keepdims=True)
    centered = inputs_f - row_mean
    variance = jnp.mean(centered * centered, axis=-1, keepdims=True)
    return centered * lax.rsqrt(variance + EPSILON) * gain_f + shift_f


def tree_allowed(query_seg, query_slot, query_valid, key_seg, key_slot, key_valid, ancestors):
    seg_ids = jnp.arange(ancestors.shape[0], dtype=jnp.int32)
    onehot = (query_seg[:, None] == seg_ids[None, :]).astype(jnp.int32)
    path_ids = jnp.sum(onehot[:, :, None] * ancestors[None, :, :], axis=1)
    linked = (
        (key_seg[None, :] == path_ids[:, 0:1])
        | (key_seg[None, :] == path_ids[:, 1:2])
        | (key_seg[None, :] == path_ids[:, 2:3])
    )
    earlier = key_slot[None, :] <= query_slot[:, None]
    usable = (key_valid[None, :] == 1) & (query_valid[:, None] == 1)
    return linked & earlier & usable | (key_slot[None, :] == query_slot[:, None])


def rotate(tensor, positions, direction):
    half_rot = ROTARY // 2
    freq = 10000.0 ** (-(jnp.arange(half_rot, dtype=jnp.float32) * 2.0 / ROTARY))
    angle = direction * positions.astype(jnp.float32)[:, None] * freq[None, :]
    cosine = jnp.cos(angle)[:, None, :]
    sine = jnp.sin(angle)[:, None, :]
    first = tensor[..., :half_rot]
    second = tensor[..., half_rot:ROTARY]
    return jnp.concatenate(
        [first * cosine - second * sine, second * cosine + first * sine, tensor[..., ROTARY:]],
        axis=-1,
    )


def body(
    residual,
    norm_gain,
    norm_shift,
    qkv_weight,
    qkv_bias,
    dense_weight,
    dense_bias,
    inner_weight,
    inner_bias,
    outer_weight,
    outer_bias,
    cotangent,
    segment,
    ancestors,
    valid_slot,
):
    f32 = jnp.float32
    bf16 = jnp.bfloat16
    tp_size = lax.axis_size("tp")
    local_rows = residual.shape[0]
    group_rows = local_rows * tp_size
    head_cols = qkv_weight.shape[2]
    head_count = head_cols // HEAD_DIM
    reach_back = (TREE_LEN - 2) // group_rows + 1
    front_rows = reach_back * group_rows
    window = front_rows + group_rows
    block_rows = min(512, group_rows)
    block_count = group_rows // block_rows
    scaling = HEAD_DIM ** (-0.5)
    base_slot = lax.axis_index("fsdp") * group_rows
    vectors = (
        lax.all_gather(norm_gain, ("fsdp", "tp"), axis=0, tiled=True),
        lax.all_gather(norm_shift, ("fsdp", "tp"), axis=0, tiled=True),
        lax.all_gather(dense_bias, ("fsdp", "tp"), axis=0, tiled=True),
        lax.all_gather(outer_bias, ("fsdp", "tp"), axis=0, tiled=True),
    )
    gain_f = vectors[0].astype(f32)
    shift_f = vectors[1].astype(f32)
    bias_sum = vectors[2].astype(f32) + vectors[3].astype(f32)
    seg_front = jnp.concatenate([jnp.zeros((front_rows,), jnp.int32), segment])
    valid_front = jnp.concatenate([jnp.zeros((front_rows,), jnp.int32), valid_slot])
    query_slot = base_slot + jnp.arange(group_rows, dtype=jnp.int32)
    query_seg = lax.dynamic_slice_in_dim(segment, base_slot, group_rows)
    query_valid = lax.dynamic_slice_in_dim(valid_slot, base_slot, group_rows)
    key_slot = base_slot - front_rows + jnp.arange(window, dtype=jnp.int32)
    key_seg = lax.dynamic_slice_in_dim(seg_front, base_slot, window)
    key_valid = lax.dynamic_slice_in_dim(valid_front, base_slot, window)

    def allowed_for():
        return tree_allowed(
            query_seg, query_slot, query_valid, key_seg, key_slot, key_valid, ancestors
        )

    def count_keys(block_num):
        return jnp.sum(allowed_for().astype(jnp.int32), axis=1) - 1

    block_ids = jnp.arange(block_count, dtype=jnp.int32)
    positions = lax.map(count_keys, block_ids).reshape(group_rows)
    inputs_f = residual.astype(f32)
    normed_local = norm_rows(inputs_f, gain_f, shift_f).astype(bf16)

    def key_window(keys_own, values_own):
        key_parts = []
        value_parts = []
        for distance in range(reach_back, 0, -1):
            got_keys, got_values = passed_along((keys_own, values_own), "fsdp", distance)
            key_parts.append(got_keys)
            value_parts.append(got_values)
        return (
            jnp.concatenate(key_parts + [keys_own], axis=0),
            jnp.concatenate(value_parts + [values_own], axis=0),
        )

    def forward_pieces():
        gathered = (
            lax.all_gather(qkv_weight, "fsdp", axis=1, tiled=True),
            lax.all_gather(qkv_bias, "fsdp", axis=1, tiled=True),
            lax.all_gather(dense_weight, "fsdp", axis=1, tiled=True),
            lax.all_gather(inner_weight, "fsdp", axis=0, tiled=True),
            lax.all_gather(inner_bias, "fsdp", axis=0, tiled=True),
            lax.all_gather(outer_weight, "fsdp", axis=1, tiled=True),
        )
        normed = lax.all_gather(normed_local, "tp", axis=0, tiled=True)
        w_qkv = gathered[0]
        mixed = (
            jnp.einsum("td,sde->ste", normed, w_qkv, preferred_element_type=f32)
            + gathered[1].astype(f32)[:, None, :]
        )
        queries = rotate(mixed[0].reshape(group_rows, head_count, HEAD_DIM), positions, 1.0).astype(
            bf16
        )
        keys_own = (
            rotate(mixed[1].reshape(group_rows, head_count, HEAD_DIM), positions, 1.0)
            .astype(bf16)
            .reshape(group_rows, head_cols)
        )
        values_own = mixed[2].astype(bf16)
        keys_win, values_win = key_window(keys_own, values_own)
        keys_win = keys_win.reshape(window, head_count, HEAD_DIM)
        values_win = values_win.reshape(window, head_count, HEAD_DIM)

        def attend(block_num):
            scores = (
                jnp.einsum("qhe,khe->hqk", queries, keys_win, preferred_element_type=f32) * scaling
            )
            scores = jnp.where(allowed_for()[None], scores, -jnp.inf)
            top_score = jnp.max(scores, axis=-1, keepdims=True)
            expo = jnp.exp(scores - top_score)
            summed = jnp.sum(expo, axis=-1, keepdims=True)
            probs_low = (expo / summed).astype(bf16)
            attended = jnp.einsum("hqk,khe->qhe", probs_low, values_win, preferred_element_type=f32)
            return (attended, (top_score + jnp.log(summed))[..., 0])

        attended, log_sums = lax.map(attend, block_ids)
        attended = attended.reshape(group_rows, head_cols).astype(bf16)
        pre_act = jnp.dot(normed, gathered[3], preferred_element_type=f32) + gathered[4].astype(f32)
        activated = jax.nn.gelu(pre_act, approximate=True).astype(bf16)
        return (
            gathered,
            normed,
            queries,
            keys_win,
            values_win,
            attended,
            log_sums,
            pre_act,
            activated,
        )

    gathered, normed, queries, keys_win, values_win, attended, log_sums, pre_act, activated = (
        forward_pieces()
    )
    partial_rows = jnp.dot(attended, gathered[2], preferred_element_type=f32) + jnp.dot(
        activated, gathered[5], preferred_element_type=f32
    )
    summed_rows = lax.psum_scatter(partial_rows, "tp", scatter_dimension=0, tiled=True)
    output = (inputs_f + summed_rows + bias_sum).astype(bf16)
    out_bias_grad = jnp.sum(cotangent.astype(f32), axis=0)
    grad_rows = lax.all_gather(cotangent, "tp", axis=0, tiled=True)
    gathered, normed, queries, keys_win, values_win, attended, log_sums, pre_act, activated = (
        forward_pieces()
    )
    w_qkv = gathered[0]
    w_dense = gathered[2]
    w_inner = gathered[3]
    w_outer = gathered[5]
    outer_grad = jnp.einsum("tf,td->fd", activated, grad_rows, preferred_element_type=f32)
    act_grad = jnp.einsum("td,fd->tf", grad_rows, w_outer, preferred_element_type=f32)
    unused_value, gelu_pull = jax.vjp(
        lambda inputs_g: jax.nn.gelu(inputs_g, approximate=True), pre_act
    )
    pre_grad = gelu_pull(act_grad)[0].astype(bf16)
    inner_grad = jnp.einsum("td,tf->df", normed, pre_grad, preferred_element_type=f32)
    inner_bias_grad = jnp.sum(pre_grad.astype(f32), axis=0)
    normed_grad = jnp.einsum("tf,df->td", pre_grad, w_inner, preferred_element_type=f32)
    dense_grad = jnp.einsum("tc,td->cd", attended, grad_rows, preferred_element_type=f32)
    attn_grad = (
        jnp.einsum("td,cd->tc", grad_rows, w_dense, preferred_element_type=f32)
        .astype(bf16)
        .reshape(group_rows, head_count, HEAD_DIM)
    )

    def attend_back(carry, inputs_b):
        key_acc, value_acc = carry
        block_num, log_block = inputs_b
        scores = jnp.einsum("qhe,khe->hqk", queries, keys_win, preferred_element_type=f32) * scaling
        probs = jnp.where(allowed_for()[None], jnp.exp(scores - log_block[..., None]), 0.0)
        probs_low = probs.astype(bf16)
        prob_grad = jnp.einsum("qhe,khe->hqk", attn_grad, values_win, preferred_element_type=f32)
        row_dot = jnp.sum(probs * prob_grad, axis=-1, keepdims=True)
        score_grad = (probs * (prob_grad - row_dot)).astype(bf16)
        query_grad = (
            jnp.einsum("hqk,khe->qhe", score_grad, keys_win, preferred_element_type=f32) * scaling
        )
        key_part = (
            key_acc
            + jnp.einsum("hqk,qhe->khe", score_grad, queries, preferred_element_type=f32) * scaling
        )
        value_part = value_acc + jnp.einsum(
            "hqk,qhe->khe", probs_low, attn_grad, preferred_element_type=f32
        )
        key_acc = key_part
        value_acc = value_part
        return ((key_acc, value_acc), query_grad)

    zero_window = jnp.zeros((window, head_count, HEAD_DIM), f32)
    (key_acc, value_acc), query_grads = lax.scan(
        attend_back, (zero_window, zero_window), (block_ids, log_sums)
    )
    key_flat = key_acc.reshape(window, head_cols)
    value_flat = value_acc.reshape(window, head_cols)
    own_key = key_flat[front_rows:]
    own_value = value_flat[front_rows:]
    for distance in range(1, reach_back + 1):
        lower = front_rows - distance * group_rows
        got_key, got_value = passed_along(
            (key_flat[lower : lower + group_rows], value_flat[lower : lower + group_rows]),
            "fsdp",
            -distance,
        )
        own_key = own_key + got_key
        own_value = own_value + got_value
    query_pre = rotate(
        query_grads.reshape(group_rows, head_count, HEAD_DIM), positions, -1.0
    ).reshape(group_rows, head_cols)
    key_pre = rotate(own_key.reshape(group_rows, head_count, HEAD_DIM), positions, -1.0).reshape(
        group_rows, head_cols
    )
    qkv_grad = jnp.stack([query_pre, key_pre, own_value]).astype(bf16)
    qkv_weight_part = jnp.einsum("td,ste->sde", normed, qkv_grad, preferred_element_type=f32)
    qkv_bias_part = jnp.sum(qkv_grad.astype(f32), axis=1)
    normed_grad = normed_grad + jnp.einsum(
        "ste,sde->td", qkv_grad, w_qkv, preferred_element_type=f32
    )
    local_grad = lax.psum_scatter(normed_grad, "tp", scatter_dimension=0, tiled=True)
    unused_norm, norm_pull = jax.vjp(norm_rows, inputs_f, gain_f, shift_f)
    input_grad, gain_grad, shift_grad = norm_pull(local_grad)
    residual_grad = (cotangent.astype(f32) + input_grad).astype(bf16)
    weight_sums = (
        lax.psum_scatter(qkv_weight_part, "fsdp", scatter_dimension=1, tiled=True),
        lax.psum_scatter(qkv_bias_part, "fsdp", scatter_dimension=1, tiled=True),
        lax.psum_scatter(dense_grad, "fsdp", scatter_dimension=1, tiled=True),
        lax.psum_scatter(inner_grad, "fsdp", scatter_dimension=0, tiled=True),
        lax.psum_scatter(inner_bias_grad, "fsdp", scatter_dimension=0, tiled=True),
        lax.psum_scatter(outer_grad, "fsdp", scatter_dimension=1, tiled=True),
    )
    vector_sums = (
        lax.psum_scatter(gain_grad, ("fsdp", "tp"), scatter_dimension=0, tiled=True),
        lax.psum_scatter(shift_grad, ("fsdp", "tp"), scatter_dimension=0, tiled=True),
        lax.psum_scatter(out_bias_grad, ("fsdp", "tp"), scatter_dimension=0, tiled=True),
    )
    return (
        output,
        residual_grad,
        vector_sums[0],
        vector_sums[1],
        weight_sums[0],
        weight_sums[1],
        weight_sums[2],
        vector_sums[2],
        weight_sums[3],
        weight_sums[4],
        weight_sums[5],
        vector_sums[2],
    )


def solution(mesh):
    return jax.shard_map(
        body,
        mesh=mesh,
        in_specs=(
            P(("fsdp", "tp"), None),
            P(("fsdp", "tp")),
            P(("fsdp", "tp")),
            P(None, "fsdp", "tp"),
            P(None, ("tp", "fsdp")),
            P("tp", "fsdp"),
            P(("fsdp", "tp")),
            P("fsdp", "tp"),
            P(("tp", "fsdp")),
            P("tp", "fsdp"),
            P(("fsdp", "tp")),
            P(("fsdp", "tp"), None),
            P(),
            P(),
            P(),
        ),
        out_specs=(
            P(("fsdp", "tp"), None),
            P(("fsdp", "tp"), None),
            P(("fsdp", "tp")),
            P(("fsdp", "tp")),
            P(None, "fsdp", "tp"),
            P(None, ("tp", "fsdp")),
            P("tp", "fsdp"),
            P(("fsdp", "tp")),
            P("fsdp", "tp"),
            P(("tp", "fsdp")),
            P("tp", "fsdp"),
            P(("fsdp", "tp")),
        ),
        check_vma=False,
    )
```

profile of v0, /device:TPU:0, one launch (start us, length us, event | category | flops | bytes accessed | tf_op | source)
XLA Modules:
  0.0 1016.9 jit_solution(10757736382496534110)
XLA Ops:
  10.7 42.2 %all-reduce.11 = (bf16[2048]{0:T(1024)(128)(2,1)S(1)}, bf16[2048]{0:T(1024)(128)(2,1)S(1)}, bf16[2048]{0:T(1024)(128)(2,1)}, bf16[2048]{0:T(1024)(128)(2,1)}) all-reduce(bf16[2048]{0:T(1024)(128)(2,1)S(1)} %dynamic-update-slice.1, bf16[2048]{0:T(1024)(128)(2,1)S(1)} %dynamic-update-slice, ...), channel_id=1, replica_groups=mesh['fsdp'=8,'tp'=4] {'fsdp','tp'}, use_global_device_ids=true, to_apply=%add.3 | all-reduce | flops 8192 | bytes 32768
  56.0 2.2 fusion.31
  58.3 2.3 copy.69
  65.6 10.2 %all-gather = bf16[8,64,3]{1,2,0:T(4,128)(2,1)S(1)} all-gather(bf16[1,64,3]{1,2,0:T(4,128)(2,1)S(1)} %bitcast.110), channel_id=1, replica_groups=mesh['fsdp'=8,'tp'=4] {'fsdp'}, dimensions={0}, use_global_device_ids=true | all-gather | bytes 3456 | tf_op jit(solution)/shard_map/all_gather | solution.py:130
  75.9 7.9 all-gather.1
  85.4 19.4 %all-gather.9.cloned.1.call-done = bf16[512,2048]{1,0:T(8,128)(2,1)} async-done(((bf16[128,2048]{1,0:T(8,128)(2,1)}), bf16[512,2048]{1,0:T(8,128)(2,1)}) %all-gather.9.cloned.1.call-update) | async-done | bytes 2097168 | tf_op jit(solution)/shard_map/all_gather | solution.py:136
  104.8 47.9 %all-gather.11.cloned.1.call-done = bf16[3,2048,512]{1,2,0:T(8,128)(2,1)} async-done(((bf16[3,256,512]{1,2,0:T(8,128)(2,1)}), bf16[3,2048,512]{1,2,0:T(8,128)(2,1)}) %all-gather.11.cloned.1.call-update) | async-done | bytes 6291472 | tf_op jit(solution)/shard_map/all_gather | solution.py:129
  152.6 6.2 add_bitcast_fusion
  160.6 4.2 collective-permute-start.2
  164.7 2.7 collective-permute-start.3
  167.4 32.8 %all-gather.19.cloned.1.call-done = bf16[512,2048]{1,0:T(8,128)(2,1)} async-done(((bf16[128,2048]{1,0:T(8,128)(2,1)}), bf16[512,2048]{1,0:T(8,128)(2,1)}) %all-gather.19.cloned.1.call-update) | async-done | bytes 2097168 | tf_op jit(solution)/shard_map/all_gather | solution.py:192
  200.2 28.7 %all-gather.13.cloned.1.call-done = bf16[512,2048]{1,0:T(8,128)(2,1)} async-done(((bf16[512,256]{1,0:T(8,128)(2,1)}), bf16[512,2048]{1,0:T(8,128)(2,1)}) %all-gather.13.cloned.1.call-update) | async-done | bytes 2097168 | tf_op jit(solution)/shard_map/all_gather | solution.py:131
  228.9 3.5 convolution_convert_fusion
  233.8 3.4 collective-permute-start
  239.4 11.9 %select_reduce_fusion = (f32[8,512]{1,0:T(8,128)S(1)}, f32[8,512,1536]{2,1,0:T(8,128)}) fusion(pred[512,1536]{1,0:T(8,128)(4,1)S(1)} %get-tuple-element.236, bf16[512,8,64]{0,2,1:T(8,128)(2,1)S(1)} %maximum_convert_fusion, bf16[512,8,64]{0,2,1:T(8,128)(2,1)} %bitcast.14, bf16[512,8,64]{0,2,1:T(8,128)(2,1)} %bitcast.13, bf16[512,8,32]{0,2,1:T(8,128)(2,1)S(1)} %slice.202, ...), kind=kOutput, calls=%fused_computation.5 | convolution fusion | flops 830468096 | bytes 28065792 | tf_op jit(solution)/shard_map/while/body/eval_jaxpr/qhe,khe->hqk/dot_general | solution.py:157
  251.3 11.6 %fusion = f32[8,512]{1,0:T(8,128)S(1)} fusion(f32[8,512,1536]{2,1,0:T(8,128)} %get-tuple-element.268, f32[8,512]{1,0:T(8,128)S(1)} %get-tuple-element.267, pred[512,1536]{1,0:T(8,128)(4,1)S(1)} %get-tuple-element.236), kind=kLoop, calls=%fused_computation.6 | loop fusion | flops 25161728 | bytes 25985024 | tf_op jit(solution)/shard_map/while/body/eval_jaxpr/reduce_sum | solution.py:162
  263.5 19.6 %multiply_reduce_fusion = (f32[8,512]{1,0:T(8,128)S(1)}, f32[8,512,1536]{2,1,0:T(8,128)}) fusion(f32[8,512,1536]{2,1,0:T(8,128)} %get-tuple-element.268, f32[8,512]{1,0:T(8,128)S(1)} %log_add_fusion, pred[512,1536]{1,0:T(8,128)(4,1)S(1)} %get-tuple-element.236, bf16[512,8,64]{0,2,1:T(8,128)(2,1)S(1)} %bitcast.100, bf16[1536,8,64]{0,2,1:T(8,128)(2,1)S(1)} %bitcast.82), kind=kOutput, calls=%fused_computation.1 | convolution fusion | flops 836759552 | bytes 53248000 | tf_op jit(solution)/shard_map/while/body/eval_jaxpr/qhe,khe->hqk/dot_general | solution.py:222
  283.1 17.4 %multiply_convert_fusion = bf16[8,512,1536]{2,1,0:T(8,128)(2,1)S(1)} fusion(f32[8,512,1536]{2,1,0:T(8,128)} %get-tuple-element.270, f32[8,512,1536]{2,1,0:T(8,128)} %get-tuple-element.268, f32[8,512]{1,0:T(8,128)S(1)} %get-tuple-element.269, f32[8,512]{1,0:T(8,128)S(1)} %log_add_fusion, pred[512,1536]{1,0:T(8,128)(4,1)S(1)} %get-tuple-element.236), kind=kLoop, calls=%fused_computation | loop fusion | flops 37748736 | bytes 63733760 | tf_op jit(solution)/shard_map/while/body/eval_jaxpr/convert_element_type | solution.py:224
  300.5 2.3 fusion.13
  302.8 2.7 copy-done
  309.8 10.9 %fusion.14 = f32[1536,8,64]{0,2,1:T(8,128)S(1)} fusion(bf16[512,8,64]{0,2,1:T(8,128)(2,1)S(1)} %bitcast.101, f32[8,512,1536]{2,1,0:T(8,128)} %get-tuple-element.268, f32[8,512]{1,0:T(8,128)S(1)} %log_add_fusion, pred[512,1536]{1,0:T(8,128)(4,1)S(1)} %get-tuple-element.236), kind=kOutput, calls=%fused_computation.26 | convolution fusion | flops 830472192 | bytes 29638656 | tf_op jit(solution)/shard_map/while/body/eval_jaxpr/hqk,qhe->khe/dot_general | solution.py:232
  322.3 2.5 copy.71
  328.8 9.0 fusion.26
  340.4 22.6 %collective-permute-done.5 = f32[512,512]{0,1:T(8,128)} collective-permute-done((f32[512,512]{0,1:T(8,128)}, f32[512,512]{0,1:T(8,128)}, u32[]{:S(2)}, u32[]{:S(2)}) %collective-permute-start.5) | collective-permute-done | bytes 1048608 | tf_op jit(solution)/shard_map/ppermute | solution.py:15
  374.3 11.8 %collective-permute-done.7 = f32[512,512]{1,0:T(8,128)} collective-permute-done((f32[512,512]{1,0:T(8,128)}, f32[512,512]{1,0:T(8,128)}, u32[]{:S(2)}, u32[]{:S(2)}) %collective-permute-start.7) | collective-permute-done | bytes 1048608 | tf_op jit(solution)/shard_map/ppermute | solution.py:15
  391.0 8.8 reduce-scatter.12.cloned.1.call-start
  399.8 10.5 %fusion.61 = f32[512,2048]{1,0:T(8,128)} fusion(bf16[512,2048]{1,0:T(8,128)(2,1)} %all-gather.9.cloned.1.call-done, bf16[2048,2048]{1,0:T(8,128)(2,1)} %all-gather.15.cloned.1.call-done), kind=kOutput, calls=%fused_computation.123 | convolution fusion | flops 4294967296 | bytes 14680064 | tf_op jit(solution)/shard_map/dot_general | solution.py:169
  410.4 9.8 all-gather.17.cloned.1.call-done
  420.2 12.2 %convert_reduce_fusion = (f32[2048]{0:T(1024)S(1)}, bf16[512,2048]{1,0:T(8,128)(2,1)S(1)}) fusion(f32[512,2048]{1,0:T(8,128)} %fusion.61, f32[2048]{0:T(1024)S(1)} %bitcast.106, bf16[512,2048]{1,0:T(8,128)(2,1)} %all-gather.19.cloned.1.call-done, bf16[2048,2048]{1,0:T(8,128)(2,1)} %all-gather.17.cloned.1.call-done), kind=kOutput, calls=%fused_computation.22 | convolution fusion | flops 4319082496 | bytes 16793600 | tf_op jit(solution)/shard_map/td,fd->tf/dot_general | solution.py:201
  432.5 4.8 fusion.62
  437.3 7.9 bitcast_add_fusion
  446.0 11.6 %fusion.27 = bf16[8,64,512]{2,1,0:T(8,128)(2,1)S(1)} fusion(bf16[1536,8,64]{0,2,1:T(8,128)(2,1)S(1)} %bitcast.83, f32[8,512,1536]{2,1,0:T(8,128)} %get-tuple-element.268, f32[8,512]{1,0:T(8,128)S(1)} %copy-done.19, f32[8,512]{1,0:T(8,128)S(1)} %get-tuple-element.267, pred[512,1536]{1,0:T(8,128)(4,1)S(1)} %get-tuple-element.236), kind=kOutput, calls=%fused_computation.51 | convolution fusion | flops 837025792 | bytes 28082176 | tf_op jit(solution)/shard_map/while/body/eval_jaxpr/hqk,khe->qhe/dot_general | solution.py:164
  457.6 8.1 fusion.54
  465.7 3.4 convolution_add_fusion
  470.3 8.0 convolution_bitcast_fusion
  479.9 3.3 fusion.63
  483.5 12.6 %fusion.64 = f32[2048,2048]{1,0:T(8,128)} fusion(bf16[512,2048]{1,0:T(8,128)(2,1)} %all-gather.9.cloned.1.call-done, bf16[512,2048]{1,0:T(8,128)(2,1)} %copy-done.37), kind=kOutput, calls=%fused_computation.126 | convolution fusion | flops 4294967296 | bytes 20971520 | tf_op jit(solution)/shard_map/td,tf->df/dot_general | solution.py:206
  496.1 11.9 %fusion.53 = f32[2048,2048]{1,0:T(8,128)} fusion(bf16[512,2048]{1,0:T(8,128)(2,1)S(1)} %copy-done.11, f32[512,2048]{1,0:T(8,128)} %fusion.61, f32[2048]{0:T(1024)S(1)} %bitcast.108), kind=kOutput, calls=%fused_computation.116 | convolution fusion | flops 4305453056 | bytes 23076864 | tf_op jit(solution)/shard_map/tf,td->fd/dot_general | solution.py:200
  511.4 14.1 %all-reduce.9 = f32[2048]{0:T(1024)S(1)} all-reduce(f32[2048]{0:T(1024)S(1)} %get-tuple-element.233), channel_id=11, replica_groups=mesh['fsdp'=8,'tp'=4] {'fsdp'}, use_global_device_ids=true, to_apply=%region_23.24.clone | all-reduce | flops 2048 | bytes 16384
  526.1 10.6 %reduce-scatter.12.cloned.1.call-done = f32[128,2048]{1,0:T(8,128)} async-done(((f32[512,2048]{1,0:T(8,128)}), f32[128,2048]{1,0:T(8,128)}) %reduce-scatter.12.cloned.1.call-update) | async-done | bytes 1048592 | tf_op jit(solution)/shard_map/reduce_scatter | solution.py:268
  540.0 76.3 %reduce-scatter.10.cloned.1.call-done = f32[128,2048]{1,0:T(8,128)} async-done(((f32[512,2048]{1,0:T(8,128)}), f32[128,2048]{1,0:T(8,128)}) %reduce-scatter.10.cloned.1.call-update) | async-done | bytes 1048592 | tf_op jit(solution)/shard_map/reduce_scatter | solution.py:189
  616.3 3.2 convert_reduce_fusion.4
  619.5 41.2 %all-reduce.10 = (f32[2048]{0:T(1024)S(1)}, f32[2048]{0:T(1024)S(1)}, f32[2048]{0:T(1024)S(1)}) all-reduce(f32[2048]{0:T(1024)S(1)} %get-tuple-element.222, f32[2048]{0:T(1024)S(1)} %get-tuple-element.224, f32[2048]{0:T(1024)S(1)} %get-tuple-element.253), channel_id=4, replica_groups=mesh['fsdp'=8,'tp'=4] {'fsdp','tp'}, use_global_device_ids=true, to_apply=%region_12.13.clone | all-reduce | flops 6144 | bytes 49152
  661.9 51.6 %reduce-scatter.14.cloned.1.call-done = f32[3,256,512]{1,2,0:T(8,128)} async-done(((f32[3,2048,512]{1,2,0:T(8,128)}), f32[3,256,512]{1,2,0:T(8,128)}) %reduce-scatter.14.cloned.1.call-update) | async-done | bytes 1572880 | tf_op jit(solution)/shard_map/reduce_scatter | solution.py:273
  713.6 3.0 copy.78
  716.6 52.6 %reduce-scatter.16.cloned.1.call-done = f32[512,256]{1,0:T(8,128)} async-done(((f32[512,2048]{1,0:T(8,128)}), f32[512,256]{1,0:T(8,128)}) %reduce-scatter.16.cloned.1.call-update) | async-done | bytes 524304 | tf_op jit(solution)/shard_map/reduce_scatter | solution.py:275
  769.2 120.0 %reduce-scatter.18.cloned.1.call-done = f32[256,2048]{1,0:T(8,128)} async-done(((f32[2048,2048]{1,0:T(8,128)}), f32[256,2048]{1,0:T(8,128)}) %reduce-scatter.18.cloned.1.call-update) | async-done | bytes 2097168 | tf_op jit(solution)/shard_map/reduce_scatter | solution.py:276
  889.2 120.2 %reduce-scatter.20.cloned.1.call-done = f32[2048,256]{1,0:T(8,128)} async-done(((f32[2048,2048]{1,0:T(8,128)}), f32[2048,256]{1,0:T(8,128)}) %reduce-scatter.20.cloned.1.call-update) | async-done | bytes 2097168 | tf_op jit(solution)/shard_map/reduce_scatter | solution.py:278
  (182 shorter events, 59.7 us)
Async XLA Ops:
  7.2 56.0 %copy-start.21 = (s32[4096]{0:T(1024)S(1)}, s32[4096]{0:T(1024)}, u32[]{:S(2)}) copy-start(s32[4096]{0:T(1024)} %param.27) | copy-start | bytes 49156
  7.2 56.1 %copy-start.20 = (s32[4096]{0:T(1024)S(1)}, s32[4096]{0:T(1024)}, u32[]{:S(2)}) copy-start(s32[4096]{0:T(1024)} %param.29) | copy-start | bytes 49156
  7.2 56.3 %copy-start.29 = (s32[39,3]{0,1:T(4,128)S(1)}, s32[39,3]{0,1:T(4,128)}, u32[]{:S(2)}) copy-start(s32[39,3]{0,1:T(4,128)} %param.28) | copy-start | bytes 1408
  7.2 97.6 %all-gather.9.cloned.1.call-start = ((), (), s32[]{:S(2)}) async-start(), calls=%async_computation.7 | async-start | bytes 2621440 | tf_op jit(solution)/shard_map/all_gather | solution.py:136
  52.9 2.6 copy-start.16
  54.1 11.5 %copy-start.30 = (bf16[3,64]{1,0:T(4,128)(2,1)S(1)}, bf16[3,64]{1,0:T(4,128)(2,1)}, u32[]{:S(2)}) copy-start(bf16[3,64]{1,0:T(4,128)(2,1)} %param.19) | copy-start | bytes 1156
  54.1 21.8 %copy-start.34 = (bf16[256]{0:T(256)(128)(2,1)S(1)}, bf16[256]{0:T(256)(128)(2,1)}, u32[]{:S(2)}) copy-start(bf16[256]{0:T(256)(128)(2,1)} %param.23) | copy-start | bytes 1540
  55.5 8.2 copy-start.31
  58.3 94.3 %all-gather.11.cloned.1.call-start = ((), (), s32[]{:S(2)}) async-start(), calls=%async_computation.8 | async-start | bytes 7077888 | tf_op jit(solution)/shard_map/all_gather | solution.py:129
  60.7 139.5 %all-gather.19.cloned.1.call-start = ((), (), s32[]{:S(2)}) async-start(), calls=%async_computation.13 | async-start | bytes 2621440 | tf_op jit(solution)/shard_map/all_gather | solution.py:192
  61.4 167.5 %all-gather.13.cloned.1.call-start = ((), (), s32[]{:S(2)}) async-start(), calls=%async_computation.9 | async-start | bytes 2359296 | tf_op jit(solution)/shard_map/all_gather | solution.py:131
  62.0 337.9 %all-gather.15.cloned.1.call-start = ((), (), s32[]{:S(2)}) async-start(), calls=%async_computation.10 | async-start | bytes 9437184 | tf_op jit(solution)/shard_map/all_gather | solution.py:132
  62.6 357.7 %all-gather.17.cloned.1.call-start = ((), (), s32[]{:S(2)}) async-start(), calls=%async_computation.11 | async-start | bytes 9437184 | tf_op jit(solution)/shard_map/all_gather | solution.py:134
  63.1 446.8 %reduce-scatter.22.cloned.1.call-start = ((), (), s32[]{:S(2)}) async-start(), calls=%async_computation.19 | async-start | bytes 294912
  160.5 78.9 %copy-start.14 = (bf16[512,8,64]{0,2,1:T(8,128)(2,1)}, bf16[512,8,64]{0,2,1:T(8,128)(2,1)S(1)}, u32[]{:S(2)}) copy-start(bf16[512,8,64]{0,2,1:T(8,128)(2,1)S(1)} %maximum_convert_fusion) | copy-start | bytes 1572868
  160.6 78.8 %collective-permute-start.2 = (bf16[512,512]{0,1:T(8,128)(2,1)S(1)}, bf16[512,512]{0,1:T(8,128)(2,1)}, u32[]{:S(2)}, u32[]{:S(2)}) collective-permute-start(bf16[512,512]{0,1:T(8,128)(2,1)S(1)} %bitcast.97), channel_id=1, source_target_pairs={{0,8},{4,12},{8,16},{12,20},{16,24},{20,28},{1,9},{5,13},{9,17},{1... | collective-permute-start | bytes 1572872 | tf_op jit(solution)/shard_map/ppermute | solution.py:15
  164.7 74.7 %collective-permute-start.3 = (bf16[512,512]{0,1:T(8,128)(2,1)S(1)}, bf16[512,512]{0,1:T(8,128)(2,1)}, u32[]{:S(2)}, u32[]{:S(2)}) collective-permute-start(bf16[512,512]{0,1:T(8,128)(2,1)S(1)} %bitcast.98), channel_id=1, source_target_pairs={{0,4},{4,8},{8,12},{12,16},{16,20},{20,24},{24,28},{1,5},{5,9},{9,... | collective-permute-start | bytes 1572872 | tf_op jit(solution)/shard_map/ppermute | solution.py:15
  233.8 29.2 %collective-permute-start = (bf16[512,512]{0,1:T(8,128)(2,1)S(1)}, bf16[512,512]{0,1:T(8,128)(2,1)S(1)}, u32[]{:S(2)}, u32[]{:S(2)}) collective-permute-start(bf16[512,512]{0,1:T(8,128)(2,1)S(1)} %fusion.41), channel_id=1, source_target_pairs={{0,8},{4,12},{8,16},{12,20},{16,24},{20,28},{1,9},{5,13},{9,17},{1... | collective-permute-start | bytes 1572872 | tf_op jit(solution)/shard_map/ppermute | solution.py:15
  237.2 25.8 %collective-permute-start.1 = (bf16[512,512]{0,1:T(8,128)(2,1)S(1)}, bf16[512,512]{0,1:T(8,128)(2,1)S(1)}, u32[]{:S(2)}, u32[]{:S(2)}) collective-permute-start(bf16[512,512]{0,1:T(8,128)(2,1)S(1)} %fusion.41), channel_id=1, source_target_pairs={{0,4},{4,8},{8,12},{12,16},{16,20},{20,24},{24,28},{1,5},{5,9},{9,... | collective-permute-start | bytes 1572872 | tf_op jit(solution)/shard_map/ppermute | solution.py:15
  300.5 5.0 copy-start
  307.2 33.2 %collective-permute-start.4 = (f32[512,512]{0,1:T(8,128)}, f32[512,512]{0,1:T(8,128)}, u32[]{:S(2)}, u32[]{:S(2)}) collective-permute-start(f32[512,512]{0,1:T(8,128)} %bitcast.23), channel_id=1, source_target_pairs={{4,0},{8,4},{12,8},{16,12},{20,16},{24,20},{28,24},{5,1},{9,5},{13... | collective-permute-start | bytes 3145736 | tf_op jit(solution)/shard_map/ppermute | solution.py:15
  308.5 54.5 %collective-permute-start.5 = (f32[512,512]{0,1:T(8,128)}, f32[512,512]{0,1:T(8,128)}, u32[]{:S(2)}, u32[]{:S(2)}) collective-permute-start(f32[512,512]{0,1:T(8,128)} %bitcast.24), channel_id=1, source_target_pairs={{8,0},{12,4},{16,8},{20,12},{24,16},{28,20},{9,1},{13,5},{17,9},{2... | collective-permute-start | bytes 3145736 | tf_op jit(solution)/shard_map/ppermute | solution.py:15
  324.9 49.4 %collective-permute-start.6 = (f32[512,512]{1,0:T(8,128)}, f32[512,512]{1,0:T(8,128)}, u32[]{:S(2)}, u32[]{:S(2)}) collective-permute-start(f32[512,512]{1,0:T(8,128)} %copy.71), channel_id=1, source_target_pairs={{4,0},{8,4},{12,8},{16,12},{20,16},{24,20},{28,24},{5,1},{9,5},{13... | collective-permute-start | bytes 3145736 | tf_op jit(solution)/shard_map/ppermute | solution.py:15
  327.5 58.6 %collective-permute-start.7 = (f32[512,512]{1,0:T(8,128)}, f32[512,512]{1,0:T(8,128)}, u32[]{:S(2)}, u32[]{:S(2)}) collective-permute-start(f32[512,512]{1,0:T(8,128)} %copy.73), channel_id=1, source_target_pairs={{8,0},{12,4},{16,8},{20,12},{24,16},{28,20},{9,1},{13,5},{17,9},{2... | collective-permute-start | bytes 3145736 | tf_op jit(solution)/shard_map/ppermute | solution.py:15
  340.4 25.6 %copy-start.3 = (f32[512,8,64]{0,2,1:T(8,128)S(1)}, f32[512,8,64]{0,2,1:T(8,128)}, u32[]{:S(2)}) copy-start(f32[512,8,64]{0,2,1:T(8,128)} %copy-done.2) | copy-start | bytes 3145732
  340.4 27.2 %copy-start.15 = (bf16[512,8,32]{0,2,1:T(8,128)(2,1)S(1)}, bf16[512,8,32]{0,2,1:T(8,128)(2,1)}, u32[]{:S(2)}) copy-start(bf16[512,8,32]{0,2,1:T(8,128)(2,1)} %slice.201) | copy-start | bytes 786436
  391.0 29.2 %copy-start.24 = (f32[8,1,256]{2,1,0:T(1,128)S(1)}, f32[8,1,256]{2,1,0:T(1,128)}, u32[]{:S(2)}) copy-start(f32[8,1,256]{2,1,0:T(1,128)} %convert_element_type.155) | copy-start | bytes 24580
  391.0 145.7 %reduce-scatter.12.cloned.1.call-start = ((), (), s32[]{:S(2)}) async-start(), calls=%async_computation.14 | async-start | bytes 5242880 | tf_op jit(solution)/shard_map/reduce_scatter | solution.py:268
  420.2 12.3 %copy-start.33 = (bf16[2048,2048]{1,0:T(8,128)(2,1)S(1)}, bf16[2048,2048]{1,0:T(8,128)(2,1)}, u32[]{:S(2)}) copy-start(bf16[2048,2048]{1,0:T(8,128)(2,1)} %all-gather.15.cloned.1.call-done) | copy-start | bytes 25165828
  432.5 4.8 copy-start.37
  432.5 4.8 copy-start.6
  432.5 4.8 copy-start.7
  432.5 4.8 copy-start.9
  445.3 171.0 %reduce-scatter.10.cloned.1.call-start = ((), (), s32[]{:S(2)}) async-start(), calls=%async_computation.12 | async-start | bytes 5242880 | tf_op jit(solution)/shard_map/reduce_scatter | solution.py:189
  446.0 11.6 %copy-start.38 = (f32[512,2048]{1,0:T(8,128)S(1)}, f32[512,2048]{1,0:T(8,128)}, u32[]{:S(2)}) copy-start(f32[512,2048]{1,0:T(8,128)} %fusion.61) | copy-start | bytes 12582916
  457.6 8.1 copy-start.13
  469.1 244.5 %reduce-scatter.14.cloned.1.call-start = ((), (), s32[]{:S(2)}) async-start(), calls=%async_computation.15 | async-start | bytes 14155776 | tf_op jit(solution)/shard_map/reduce_scatter | solution.py:273
  478.3 290.9 %reduce-scatter.16.cloned.1.call-start = ((), (), s32[]{:S(2)}) async-start(), calls=%async_computation.16 | async-start | bytes 4718592 | tf_op jit(solution)/shard_map/reduce_scatter | solution.py:275
  483.2 406.1 %reduce-scatter.18.cloned.1.call-start = ((), (), s32[]{:S(2)}) async-start(), calls=%async_computation.17 | async-start | bytes 18874368 | tf_op jit(solution)/shard_map/reduce_scatter | solution.py:276
  496.1 513.3 %reduce-scatter.20.cloned.1.call-start = ((), (), s32[]{:S(2)}) async-start(), calls=%async_computation.18 | async-start | bytes 18874368 | tf_op jit(solution)/shard_map/reduce_scatter | solution.py:278
  508.0 1.9 copy-start.28
  508.0 28.7 %copy-start.1 = (bf16[128,2048]{1,0:T(8,128)(2,1)S(1)}, bf16[128,2048]{1,0:T(8,128)(2,1)}, u32[]{:S(2)}) copy-start(bf16[128,2048]{1,0:T(8,128)(2,1)} %param.15) | copy-start | bytes 1572868
  508.0 28.7 %copy-start.17 = (f32[2048]{0:T(1024)S(1)}, f32[2048]{0:T(1024)}, u32[]{:S(2)}) copy-start(f32[2048]{0:T(1024)} %copy-done.16) | copy-start | bytes 24580
  508.0 28.7 %copy-start.23 = (f32[128]{0:T(128)S(1)}, f32[128]{0:T(128)}, u32[]{:S(2)}) copy-start(f32[128]{0:T(128)} %copy-done.22) | copy-start | bytes 1540
  508.0 30.2 %copy-start.32 = (f32[128]{0:T(128)S(1)}, f32[128]{0:T(128)}, u32[]{:S(2)}) copy-start(f32[128]{0:T(128)} %copy-done.31) | copy-start | bytes 1540
  508.0 30.2 %copy-start.26 = (f32[128]{0:T(128)S(1)}, f32[128]{0:T(128)}, u32[]{:S(2)}) copy-start(f32[128]{0:T(128)} %copy-done.25) | copy-start | bytes 1540
  508.1 108.2 %copy-start.12 = (bf16[128,2048]{1,0:T(8,128)(2,1)S(1)}, bf16[128,2048]{1,0:T(8,128)(2,1)}, u32[]{:S(2)}) copy-start(bf16[128,2048]{1,0:T(8,128)(2,1)} %param.26) | copy-start | bytes 1572868
  660.7 349.2 %copy-start.36 = (f32[64]{0:T(128)}, f32[64]{0:T(128)S(1)}, u32[]{:S(2)}) copy-start(f32[64]{0:T(128)S(1)} %dynamic-slice.2) | copy-start | bytes 772
  (12 other events, 13.1 us)
Sparse Core Ops, SparseCore 0:
  58.4 46.3 all-gather.8
  107.2 45.3 all-gather.10
  154.2 45.9 all-gather.18
  201.9 26.8 all-gather.12
  230.6 64.4 all-gather.14
  296.8 123.3 all-gather.16
  423.8 33.6 reduce-scatter.21
  459.9 76.7 reduce-scatter.11
  539.0 77.2 reduce-scatter.9
  620.0 93.4 reduce-scatter.13
  717.9 51.3 reduce-scatter.15
  773.2 115.9 reduce-scatter.17
  893.4 115.9 reduce-scatter.19
where the time goes:
time: 1020 us
  waiting for transfers between devices  607 us (60%)
  matrix products  158 us (15%)
  blocking collectives  116 us (11%)
  other arithmetic  54 us (5%)
  local copies, waits for them, and re-layouts  40 us (4%)
  starting transfers between devices  27.1 us (3%)
  between operations  15.8 us (2%)
    reduce_scatter x1, waiting for transfers between devices, body(): lax.psum_scatter(outer_grad, 'fsdp', scatter_dimension=1, tiled=True)  120 us
    reduce_scatter x1, waiting for transfers between devices, body(): lax.psum_scatter(inner_grad, 'fsdp', scatter_dimension=0, tiled=True)  120 us
    unnamed x3, blocking collectives  97.5 us
    reduce_scatter x1, waiting for transfers between devices, body(): lax.psum_scatter(partial_rows, 'tp', scatter_dimension=0, tiled=True)  76.3 us
    reduce_scatter x1, waiting for transfers between devices, body(): lax.psum_scatter(dense_grad, 'fsdp', scatter_dimension=1, tiled=True)  52.6 us
    reduce_scatter x1, waiting for transfers between devices, body(): lax.psum_scatter(qkv_weight_part, 'fsdp', scatter_dimension=1, tiled=True)  51.6 us
    all_gather x1, waiting for transfers between devices, forward_pieces(): lax.all_gather(qkv_weight, 'fsdp', axis=1, tiled=True)  47.9 us
    ppermute x8, waiting for transfers between devices, passed_along(): lax.ppermute(value, axis, [(source, source + steps) for source in range(i...  34.4 us
  transfers between devices with their start and end apart: 21, of which 13 were waited for; matrix products, arithmetic and copies ran while one was open for 23% of the time, Pallas kernels for 0%

commit v1 on v0

--- a/solution.py
+++ b/solution.py
@@ -189,7 +189,12 @@
     summed_rows = lax.psum_scatter(partial_rows, "tp", scatter_dimension=0, tiled=True)
     output = (inputs_f + summed_rows + bias_sum).astype(bf16)
     out_bias_grad = jnp.sum(cotangent.astype(f32), axis=0)
-    grad_rows = lax.all_gather(cotangent, "tp", axis=0, tiled=True)
+    ring = [cotangent]
+    for hop in range(3):
+        ring.append(lax.ppermute(ring[-1], "tp", [(dev, (dev + 1) % 4) for dev in range(4)]))
+    grad_rows = jnp.roll(
+        jnp.concatenate(ring[::-1], axis=0), (lax.axis_index("tp") + 1) * ring[0].shape[0], axis=0
+    )
     gathered, normed, queries, keys_win, values_win, attended, log_sums, pre_act, activated = (
         forward_pieces()
     )

time: 1020 us -> 1000 us (0.980)
  waiting for transfers between devices: 607 us -> 563 us
  starting transfers between devices: 27.1 us -> 41 us
    ppermute x0 -> x3, waiting for transfers between devices: none -> 34.3 us  [body(): lax.ppermute(ring[-1], 'tp', [(dev, (dev + 1) % 4) for dev in range(4)])]
    all_gather x1 -> x0, waiting for transfers between devices: 32.8 us -> none  [body(): grad_rows = lax.all_gather(cotangent, 'tp', axis=0, tiled=True)]
    all_gather x1, waiting for transfers between devices: 19.4 us -> 0.01 us  [forward_pieces(): normed = lax.all_gather(normed_local, 'tp', axis=0, tiled=True)]
    all_gather x1, waiting for transfers between devices: 47.9 us -> 30.4 us  [forward_pieces(): lax.all_gather(qkv_weight, 'fsdp', axis=1, tiled=True)]
    ppermute x0 -> x3, starting transfers between devices: none -> 15.1 us  [body(): lax.ppermute(ring[-1], 'tp', [(dev, (dev + 1) % 4) for dev in range(4)])]
    all_gather x1, waiting for transfers between devices: 9.85 us -> 20.7 us  [forward_pieces(): lax.all_gather(outer_weight, 'fsdp', axis=1, tiled=True)]
    unnamed x97 -> x106, local copies, waits for them, and re-layouts: 23.9 us -> 29.1 us
  transfers between devices with their start and end apart: 21 -> 23, of which waited for: 13 -> 14; matrix products, arithmetic and copies ran while one was open for 23% -> 24% of each run, Pallas kernels for 0% -> 0%
where the time goes in v1:
time: 1000 us; the launch traced here: 995 us
  waiting for transfers between devices  563 us (56%)
  matrix products  159 us (16%)
  blocking collectives  116 us (12%)
  other arithmetic  54.1 us (5%)
  local copies, waits for them, and re-layouts  46 us (5%)
  starting transfers between devices  41 us (4%)
  between operations  16.1 us (2%)
    reduce_scatter x1, waiting for transfers between devices, body(): lax.psum_scatter(outer_grad, 'fsdp', scatter_dimension=1, tiled=True)  120 us
    reduce_scatter x1, waiting for transfers between devices, body(): lax.psum_scatter(inner_grad, 'fsdp', scatter_dimension=0, tiled=True)  120 us
    unnamed x3, blocking collectives  97.5 us
    reduce_scatter x1, waiting for transfers between devices, body(): lax.psum_scatter(partial_rows, 'tp', scatter_dimension=0, tiled=True)  76.2 us
    reduce_scatter x1, waiting for transfers between devices, body(): lax.psum_scatter(dense_grad, 'fsdp', scatter_dimension=1, tiled=True)  52.5 us
    reduce_scatter x1, waiting for transfers between devices, body(): lax.psum_scatter(qkv_weight_part, 'fsdp', scatter_dimension=1, tiled=True)  51.8 us
    ppermute x3, waiting for transfers between devices, body(): lax.ppermute(ring[-1], 'tp', [(dev, (dev + 1) % 4) for dev in range(4)])  34.3 us
    all_gather x1, waiting for transfers between devices, forward_pieces(): lax.all_gather(qkv_weight, 'fsdp', axis=1, tiled=True)  30.4 us
  transfers between devices with their start and end apart: 23, of which 14 were waited for; matrix products, arithmetic and copies ran while one was open for 24% of the time, Pallas kernels for 0%

profile of v1, /device:TPU:0, one launch (start us, length us, event | category | flops | bytes accessed | tf_op | source)
XLA Modules:
  0.0 994.8 jit_solution(17308605548834277114)
XLA Ops:
  10.8 42.2 %all-reduce.11 = (bf16[2048]{0:T(1024)(128)(2,1)S(1)}, bf16[2048]{0:T(1024)(128)(2,1)S(1)}, bf16[2048]{0:T(1024)(128)(2,1)}, bf16[2048]{0:T(1024)(128)(2,1)}) all-reduce(bf16[2048]{0:T(1024)(128)(2,1)S(1)} %dynamic-update-slice.1, bf16[2048]{0:T(1024)(128)(2,1)S(1)} %dynamic-update-slice, ...), channel_id=1, replica_groups=mesh['fsdp'=8,'tp'=4] {'fsdp','tp'}, use_global_device_ids=true, to_apply=%add.3 | all-reduce | flops 8192 | bytes 32768
  57.9 2.3 copy.69
  63.6 10.2 %all-gather = bf16[8,64,3]{1,2,0:T(4,128)(2,1)S(1)} all-gather(bf16[1,64,3]{1,2,0:T(4,128)(2,1)S(1)} %bitcast.106), channel_id=1, replica_groups=mesh['fsdp'=8,'tp'=4] {'fsdp'}, dimensions={0}, use_global_device_ids=true | all-gather | bytes 3456 | tf_op jit(solution)/shard_map/all_gather | solution.py:130
  73.9 7.9 all-gather.1
  84.5 7.1 collective-permute-start.5
  93.5 20.9 %collective-permute-done.5 = bf16[128,2048]{1,0:T(8,128)(2,1)S(1)} collective-permute-done((bf16[128,2048]{1,0:T(8,128)(2,1)S(1)}, bf16[128,2048]{1,0:T(8,128)(2,1)S(1)}, u32[]{:S(2)}, u32[]{:S(2)}) %collective-permute-start.5) | collective-permute-done | bytes 524320 | tf_op jit(solution)/shard_map/ppermute | solution.py:194
  114.4 6.5 collective-permute-start.6
  121.8 11.4 %collective-permute-done.6 = bf16[128,2048]{1,0:T(8,128)(2,1)S(1)} collective-permute-done((bf16[128,2048]{1,0:T(8,128)(2,1)S(1)}, bf16[128,2048]{1,0:T(8,128)(2,1)S(1)}, u32[]{:S(2)}, u32[]{:S(2)}) %collective-permute-start.6) | collective-permute-done | bytes 524320 | tf_op jit(solution)/shard_map/ppermute | solution.py:194
  140.0 30.4 %all-gather.10.cloned.1.call-done = bf16[3,2048,512]{1,2,0:T(8,128)(2,1)} async-done(((bf16[3,256,512]{1,2,0:T(8,128)(2,1)}), bf16[3,2048,512]{1,2,0:T(8,128)(2,1)}) %all-gather.10.cloned.1.call-update) | async-done | bytes 6291472 | tf_op jit(solution)/shard_map/all_gather | solution.py:129
  170.5 6.2 add_bitcast_fusion
  178.4 4.2 collective-permute-start.2
  182.5 2.7 collective-permute-start.3
  185.2 20.9 %all-gather.12.cloned.1.call-done = bf16[512,2048]{1,0:T(8,128)(2,1)} async-done(((bf16[512,256]{1,0:T(8,128)(2,1)}), bf16[512,2048]{1,0:T(8,128)(2,1)}) %all-gather.12.cloned.1.call-update) | async-done | bytes 2097168 | tf_op jit(solution)/shard_map/all_gather | solution.py:131
  206.2 3.5 fusion.37
  211.1 2.3 collective-permute-start
  215.6 12.0 %select_reduce_fusion = (f32[8,512]{1,0:T(8,128)S(1)}, f32[8,512,1536]{2,1,0:T(8,128)}) fusion(pred[512,1536]{1,0:T(8,128)(4,1)S(1)} %get-tuple-element.234, bf16[512,8,64]{0,2,1:T(8,128)(2,1)S(1)} %maximum_convert_fusion, bf16[512,8,64]{0,2,1:T(8,128)(2,1)} %bitcast.14, bf16[512,8,64]{0,2,1:T(8,128)(2,1)} %bitcast.13, bf16[512,8,32]{0,2,1:T(8,128)(2,1)S(1)} %slice.202, ...), kind=kOutput, calls=%fused_computation.5 | convolution fusion | flops 830468096 | bytes 28065792 | tf_op jit(solution)/shard_map/while/body/eval_jaxpr/qhe,khe->hqk/dot_general | solution.py:157
  227.5 11.6 %fusion = f32[8,512]{1,0:T(8,128)S(1)} fusion(f32[8,512,1536]{2,1,0:T(8,128)} %get-tuple-element.266, f32[8,512]{1,0:T(8,128)S(1)} %get-tuple-element.265, pred[512,1536]{1,0:T(8,128)(4,1)S(1)} %get-tuple-element.234), kind=kLoop, calls=%fused_computation.6 | loop fusion | flops 25161728 | bytes 25985024 | tf_op jit(solution)/shard_map/while/body/eval_jaxpr/reduce_sum | solution.py:162
  239.7 19.6 %multiply_reduce_fusion = (f32[8,512]{1,0:T(8,128)S(1)}, f32[8,512,1536]{2,1,0:T(8,128)}) fusion(f32[8,512,1536]{2,1,0:T(8,128)} %get-tuple-element.266, f32[8,512]{1,0:T(8,128)S(1)} %log_add_fusion, pred[512,1536]{1,0:T(8,128)(4,1)S(1)} %get-tuple-element.234, bf16[512,8,64]{0,2,1:T(8,128)(2,1)S(1)} %bitcast.96, bf16[1536,8,64]{0,2,1:T(8,128)(2,1)S(1)} %bitcast.78), kind=kOutput, calls=%fused_computation.1 | convolution fusion | flops 836759552 | bytes 53248000 | tf_op jit(solution)/shard_map/while/body/eval_jaxpr/qhe,khe->hqk/dot_general | solution.py:227
  259.3 17.5 %multiply_convert_fusion = bf16[8,512,1536]{2,1,0:T(8,128)(2,1)S(1)} fusion(f32[8,512,1536]{2,1,0:T(8,128)} %get-tuple-element.268, f32[8,512,1536]{2,1,0:T(8,128)} %get-tuple-element.266, f32[8,512]{1,0:T(8,128)S(1)} %get-tuple-element.267, f32[8,512]{1,0:T(8,128)S(1)} %log_add_fusion, pred[512,1536]{1,0:T(8,128)(4,1)S(1)} %get-tuple-element.234), kind=kLoop, calls=%fused_computation | loop fusion | flops 37748736 | bytes 63733760 | tf_op jit(solution)/shard_map/while/body/eval_jaxpr/convert_element_type | solution.py:229
  276.8 2.3 fusion.13
  279.1 2.3 copy-done
  285.7 10.9 %fusion.14 = f32[1536,8,64]{0,2,1:T(8,128)S(1)} fusion(bf16[512,8,64]{0,2,1:T(8,128)(2,1)S(1)} %bitcast.97, f32[8,512,1536]{2,1,0:T(8,128)} %get-tuple-element.266, f32[8,512]{1,0:T(8,128)S(1)} %log_add_fusion, pred[512,1536]{1,0:T(8,128)(4,1)S(1)} %get-tuple-element.234), kind=kOutput, calls=%fused_computation.26 | convolution fusion | flops 830472192 | bytes 29638656 | tf_op jit(solution)/shard_map/while/body/eval_jaxpr/hqk,qhe->khe/dot_general | solution.py:237
  298.3 2.5 copy.73
  304.7 9.0 fusion.26
  316.3 24.3 %collective-permute-done.8 = f32[512,512]{0,1:T(8,128)} collective-permute-done((f32[512,512]{0,1:T(8,128)}, f32[512,512]{0,1:T(8,128)}, u32[]{:S(2)}, u32[]{:S(2)}) %collective-permute-start.8) | collective-permute-done | bytes 1048608 | tf_op jit(solution)/shard_map/ppermute | solution.py:15
  357.5 8.8 reduce-scatter.12.cloned.1.call-start
  366.4 10.9 %fusion.76 = f32[512,2048]{1,0:T(8,128)} fusion(bf16[512,2048]{1,0:T(8,128)(2,1)} %all-gather.8.cloned.1.call-done, bf16[2048,2048]{1,0:T(8,128)(2,1)} %all-gather.14.cloned.1.call-done), kind=kOutput, calls=%fused_computation.142 | convolution fusion | flops 4294967296 | bytes 14680064 | tf_op jit(solution)/shard_map/dot_general | solution.py:169
  377.3 20.7 %all-gather.16.cloned.1.call-done = bf16[2048,2048]{1,0:T(8,128)(2,1)} async-done(((bf16[2048,256]{1,0:T(8,128)(2,1)}), bf16[2048,2048]{1,0:T(8,128)(2,1)}) %all-gather.16.cloned.1.call-update) | async-done | bytes 8388624 | tf_op jit(solution)/shard_map/all_gather | solution.py:134
  398.0 12.2 %convert_reduce_fusion = (f32[2048]{0:T(1024)S(1)}, bf16[512,2048]{1,0:T(8,128)(2,1)S(1)}) fusion(f32[512,2048]{1,0:T(8,128)} %fusion.76, f32[2048]{0:T(1024)S(1)} %bitcast.102, bf16[2048,2048]{1,0:T(8,128)(2,1)} %all-gather.16.cloned.1.call-done, bf16[1024,2048]{1,0:T(8,128)(2,1)} %constant_dynamic-update-slice_fusion, s32[]{:T(128)S(6)} %select_n.36), kind=kOutput, calls=%fused_computation.22 | convolution fusion | flops 4319082496 | bytes 16793604 | tf_op jit(solution)/shard_map/td,fd->tf/dot_general | solution.py:206
  410.3 4.8 fusion.77
  415.1 7.9 bitcast_add_fusion
  423.7 11.6 %fusion.40 = bf16[8,64,512]{2,1,0:T(8,128)(2,1)S(1)} fusion(bf16[1536,8,64]{0,2,1:T(8,128)(2,1)S(1)} %bitcast.79, f32[8,512,1536]{2,1,0:T(8,128)} %get-tuple-element.266, f32[8,512]{1,0:T(8,128)S(1)} %copy-done.19, f32[8,512]{1,0:T(8,128)S(1)} %get-tuple-element.265, pred[512,1536]{1,0:T(8,128)(4,1)S(1)} %get-tuple-element.234), kind=kOutput, calls=%fused_computation.59 | convolution fusion | flops 837025792 | bytes 28082176 | tf_op jit(solution)/shard_map/while/body/eval_jaxpr/hqk,khe->qhe/dot_general | solution.py:164
  435.3 8.1 fusion.70
  443.4 3.4 convolution_add_fusion
  448.0 7.9 convolution_bitcast_fusion
  456.0 4.9 fusion.29
  461.2 14.0 %fusion.27 = f32[2048,2048]{1,0:T(8,128)} fusion(bf16[1024,2048]{1,0:T(8,128)(2,1)} %constant_dynamic-update-slice_fusion, s32[]{:T(128)S(6)} %select_n.36, f32[512,2048]{1,0:T(8,128)} %fusion.76, f32[2048]{0:T(1024)S(1)} %bitcast.104), kind=kOutput, calls=%fused_computation.48 | convolution fusion | flops 4305453056 | bytes 23076868 | tf_op jit(solution)/shard_map/tf,td->fd/dot_general | solution.py:205
  476.8 9.8 fusion.78
  489.9 14.1 %all-reduce.9 = f32[2048]{0:T(1024)S(1)} all-reduce(f32[2048]{0:T(1024)S(1)} %get-tuple-element.269), channel_id=11, replica_groups=mesh['fsdp'=8,'tp'=4] {'fsdp'}, use_global_device_ids=true, to_apply=%region_23.24.clone | all-reduce | flops 2048 | bytes 16384
  504.6 9.6 reduce-scatter.12.cloned.1.call-done
  517.6 76.2 %reduce-scatter.10.cloned.1.call-done = f32[128,2048]{1,0:T(8,128)} async-done(((f32[512,2048]{1,0:T(8,128)}), f32[128,2048]{1,0:T(8,128)}) %reduce-scatter.10.cloned.1.call-update) | async-done | bytes 1048592 | tf_op jit(solution)/shard_map/reduce_scatter | solution.py:189
  593.9 3.2 convert_reduce_fusion.4
  597.0 41.2 %all-reduce.10 = (f32[2048]{0:T(1024)S(1)}, f32[2048]{0:T(1024)S(1)}, f32[2048]{0:T(1024)S(1)}) all-reduce(f32[2048]{0:T(1024)S(1)} %get-tuple-element.222, f32[2048]{0:T(1024)S(1)} %get-tuple-element.224, f32[2048]{0:T(1024)S(1)} %get-tuple-element.251), channel_id=4, replica_groups=mesh['fsdp'=8,'tp'=4] {'fsdp','tp'}, use_global_device_ids=true, to_apply=%region_12.13.clone | all-reduce | flops 6144 | bytes 49152
  639.5 51.8 %reduce-scatter.14.cloned.1.call-done = f32[3,256,512]{1,2,0:T(8,128)} async-done(((f32[3,2048,512]{1,2,0:T(8,128)}), f32[3,256,512]{1,2,0:T(8,128)}) %reduce-scatter.14.cloned.1.call-update) | async-done | bytes 1572880 | tf_op jit(solution)/shard_map/reduce_scatter | solution.py:278
  691.3 3.0 copy.78
  694.4 52.5 %reduce-scatter.16.cloned.1.call-done = f32[512,256]{1,0:T(8,128)} async-done(((f32[512,2048]{1,0:T(8,128)}), f32[512,256]{1,0:T(8,128)}) %reduce-scatter.16.cloned.1.call-update) | async-done | bytes 524304 | tf_op jit(solution)/shard_map/reduce_scatter | solution.py:280
  746.8 120.2 %reduce-scatter.20.cloned.1.call-done = f32[2048,256]{1,0:T(8,128)} async-done(((f32[2048,2048]{1,0:T(8,128)}), f32[2048,256]{1,0:T(8,128)}) %reduce-scatter.20.cloned.1.call-update) | async-done | bytes 2097168 | tf_op jit(solution)/shard_map/reduce_scatter | solution.py:283
  867.0 120.0 %reduce-scatter.18.cloned.1.call-done = f32[256,2048]{1,0:T(8,128)} async-done(((f32[2048,2048]{1,0:T(8,128)}), f32[256,2048]{1,0:T(8,128)}) %reduce-scatter.18.cloned.1.call-update) | async-done | bytes 2097168 | tf_op jit(solution)/shard_map/reduce_scatter | solution.py:281
  (195 shorter events, 71.2 us)
Async XLA Ops:
  7.2 54.4 %copy-start.2 = (bf16[128,2048]{1,0:T(8,128)(2,1)S(1)}, bf16[128,2048]{1,0:T(8,128)(2,1)}, u32[]{:S(2)}) copy-start(bf16[128,2048]{1,0:T(8,128)(2,1)} %param.26) | copy-start | bytes 1572868
  7.2 56.1 %copy-start.21 = (s32[4096]{0:T(1024)S(1)}, s32[4096]{0:T(1024)}, u32[]{:S(2)}) copy-start(s32[4096]{0:T(1024)} %param.27) | copy-start | bytes 49156
  7.2 56.2 %copy-start.20 = (s32[4096]{0:T(1024)S(1)}, s32[4096]{0:T(1024)}, u32[]{:S(2)}) copy-start(s32[4096]{0:T(1024)} %param.29) | copy-start | bytes 49156
  7.2 56.4 %copy-start.30 = (bf16[3,64]{1,0:T(4,128)(2,1)S(1)}, bf16[3,64]{1,0:T(4,128)(2,1)}, u32[]{:S(2)}) copy-start(bf16[3,64]{1,0:T(4,128)(2,1)} %param.19) | copy-start | bytes 1156
  7.2 66.7 %copy-start.35 = (bf16[256]{0:T(256)(128)(2,1)S(1)}, bf16[256]{0:T(256)(128)(2,1)}, u32[]{:S(2)}) copy-start(bf16[256]{0:T(256)(128)(2,1)} %param.23) | copy-start | bytes 1540
  7.2 75.2 %copy-start.29 = (s32[39,3]{0,1:T(4,128)S(1)}, s32[39,3]{0,1:T(4,128)}, u32[]{:S(2)}) copy-start(s32[39,3]{0,1:T(4,128)} %param.28) | copy-start | bytes 1408
  7.2 132.8 %all-gather.8.cloned.1.call-start = ((), (), s32[]{:S(2)}) async-start(), calls=%async_computation.7 | async-start | bytes 2621440 | tf_op jit(solution)/shard_map/all_gather | solution.py:136
  54.2 37.4 %copy-start.22 = (f32[128]{0:T(128)}, f32[128]{0:T(128)S(1)}, u32[]{:S(2)}) copy-start(f32[128]{0:T(128)S(1)} %broadcast_multiply_fusion.1) | copy-start | bytes 1540
  55.6 18.3 %copy-start.31 = (f32[128]{0:T(128)}, f32[128]{0:T(128)S(1)}, u32[]{:S(2)}) copy-start(f32[128]{0:T(128)S(1)} %fusion.47) | copy-start | bytes 1540
  55.6 7.7 copy-start.25
  57.9 112.6 %all-gather.10.cloned.1.call-start = ((), (), s32[]{:S(2)}) async-start(), calls=%async_computation.8 | async-start | bytes 7077888 | tf_op jit(solution)/shard_map/all_gather | solution.py:129
  60.2 145.9 %all-gather.12.cloned.1.call-start = ((), (), s32[]{:S(2)}) async-start(), calls=%async_computation.9 | async-start | bytes 2359296 | tf_op jit(solution)/shard_map/all_gather | solution.py:131
  61.0 305.4 %all-gather.14.cloned.1.call-start = ((), (), s32[]{:S(2)}) async-start(), calls=%async_computation.10 | async-start | bytes 9437184 | tf_op jit(solution)/shard_map/all_gather | solution.py:132
  61.5 336.4 %all-gather.16.cloned.1.call-start = ((), (), s32[]{:S(2)}) async-start(), calls=%async_computation.11 | async-start | bytes 9437184 | tf_op jit(solution)/shard_map/all_gather | solution.py:134
  61.6 22.9 %collective-permute-start.4 = (bf16[128,2048]{1,0:T(8,128)(2,1)S(1)}, bf16[128,2048]{1,0:T(8,128)(2,1)S(1)}, u32[]{:S(2)}, u32[]{:S(2)}) collective-permute-start(bf16[128,2048]{1,0:T(8,128)(2,1)S(1)} %copy-done.2), channel_id=1, source_target_pairs={{0,1},{1,2},{2,3},{3,0},{4,5},{5,6},{6,7},{7,4},{8,9},{9,10},{10,1... | collective-permute-start | bytes 1572872 | tf_op jit(solution)/shard_map/ppermute | solution.py:194
  63.2 425.3 %reduce-scatter.22.cloned.1.call-start = ((), (), s32[]{:S(2)}) async-start(), calls=%async_computation.18 | async-start | bytes 294912
  84.5 29.9 %collective-permute-start.5 = (bf16[128,2048]{1,0:T(8,128)(2,1)S(1)}, bf16[128,2048]{1,0:T(8,128)(2,1)S(1)}, u32[]{:S(2)}, u32[]{:S(2)}) collective-permute-start(bf16[128,2048]{1,0:T(8,128)(2,1)S(1)} %collective-permute-done.4), channel_id=1, source_target_pairs={{0,1},{1,2},{2,3},{3,0},{4,5},{5,6},{6,7},{7,4},{8,9},{9,10},{10,1... | collective-permute-start | bytes 1572872 | tf_op jit(solution)/shard_map/ppermute | solution.py:194
  114.4 18.8 %collective-permute-start.6 = (bf16[128,2048]{1,0:T(8,128)(2,1)S(1)}, bf16[128,2048]{1,0:T(8,128)(2,1)S(1)}, u32[]{:S(2)}, u32[]{:S(2)}) collective-permute-start(bf16[128,2048]{1,0:T(8,128)(2,1)S(1)} %collective-permute-done.5), channel_id=1, source_target_pairs={{0,1},{1,2},{2,3},{3,0},{4,5},{5,6},{6,7},{7,4},{8,9},{9,10},{10,1... | collective-permute-start | bytes 1572872 | tf_op jit(solution)/shard_map/ppermute | solution.py:194
  178.4 37.2 %copy-start.14 = (bf16[512,8,64]{0,2,1:T(8,128)(2,1)}, bf16[512,8,64]{0,2,1:T(8,128)(2,1)S(1)}, u32[]{:S(2)}) copy-start(bf16[512,8,64]{0,2,1:T(8,128)(2,1)S(1)} %maximum_convert_fusion) | copy-start | bytes 1572868
  178.4 37.1 %collective-permute-start.2 = (bf16[512,512]{0,1:T(8,128)(2,1)S(1)}, bf16[512,512]{0,1:T(8,128)(2,1)}, u32[]{:S(2)}, u32[]{:S(2)}) collective-permute-start(bf16[512,512]{0,1:T(8,128)(2,1)S(1)} %bitcast.93), channel_id=1, source_target_pairs={{0,8},{4,12},{8,16},{12,20},{16,24},{20,28},{1,9},{5,13},{9,17},{1... | collective-permute-start | bytes 1572872 | tf_op jit(solution)/shard_map/ppermute | solution.py:15
  182.5 33.0 %collective-permute-start.3 = (bf16[512,512]{0,1:T(8,128)(2,1)S(1)}, bf16[512,512]{0,1:T(8,128)(2,1)}, u32[]{:S(2)}, u32[]{:S(2)}) collective-permute-start(bf16[512,512]{0,1:T(8,128)(2,1)S(1)} %bitcast.94), channel_id=1, source_target_pairs={{0,4},{4,8},{8,12},{12,16},{16,20},{20,24},{24,28},{1,5},{5,9},{9,... | collective-permute-start | bytes 1572872 | tf_op jit(solution)/shard_map/ppermute | solution.py:15
  211.1 28.1 %collective-permute-start = (bf16[512,512]{0,1:T(8,128)(2,1)S(1)}, bf16[512,512]{0,1:T(8,128)(2,1)S(1)}, u32[]{:S(2)}, u32[]{:S(2)}) collective-permute-start(bf16[512,512]{0,1:T(8,128)(2,1)S(1)} %fusion.54), channel_id=1, source_target_pairs={{0,8},{4,12},{8,16},{12,20},{16,24},{20,28},{1,9},{5,13},{9,17},{1... | collective-permute-start | bytes 1572872 | tf_op jit(solution)/shard_map/ppermute | solution.py:15
  213.4 25.8 %collective-permute-start.1 = (bf16[512,512]{0,1:T(8,128)(2,1)S(1)}, bf16[512,512]{0,1:T(8,128)(2,1)S(1)}, u32[]{:S(2)}, u32[]{:S(2)}) collective-permute-start(bf16[512,512]{0,1:T(8,128)(2,1)S(1)} %fusion.54), channel_id=1, source_target_pairs={{0,4},{4,8},{8,12},{12,16},{16,20},{20,24},{24,28},{1,5},{5,9},{9,... | collective-permute-start | bytes 1572872 | tf_op jit(solution)/shard_map/ppermute | solution.py:15
  283.1 33.2 %collective-permute-start.7 = (f32[512,512]{0,1:T(8,128)}, f32[512,512]{0,1:T(8,128)}, u32[]{:S(2)}, u32[]{:S(2)}) collective-permute-start(f32[512,512]{0,1:T(8,128)} %bitcast.23), channel_id=1, source_target_pairs={{4,0},{8,4},{12,8},{16,12},{20,16},{24,20},{28,24},{5,1},{9,5},{13... | collective-permute-start | bytes 3145736 | tf_op jit(solution)/shard_map/ppermute | solution.py:15
  284.4 56.2 %collective-permute-start.8 = (f32[512,512]{0,1:T(8,128)}, f32[512,512]{0,1:T(8,128)}, u32[]{:S(2)}, u32[]{:S(2)}) collective-permute-start(f32[512,512]{0,1:T(8,128)} %bitcast.24), channel_id=1, source_target_pairs={{8,0},{12,4},{16,8},{20,12},{24,16},{28,20},{9,1},{13,5},{17,9},{2... | collective-permute-start | bytes 3145736 | tf_op jit(solution)/shard_map/ppermute | solution.py:15
  300.8 51.8 %collective-permute-start.10 = (f32[512,512]{1,0:T(8,128)}, f32[512,512]{1,0:T(8,128)}, u32[]{:S(2)}, u32[]{:S(2)}) collective-permute-start(f32[512,512]{1,0:T(8,128)} %copy.73), channel_id=1, source_target_pairs={{8,0},{12,4},{16,8},{20,12},{24,16},{28,20},{9,1},{13,5},{17,9},{2... | collective-permute-start | bytes 3145736 | tf_op jit(solution)/shard_map/ppermute | solution.py:15
  303.4 49.2 %collective-permute-start.9 = (f32[512,512]{1,0:T(8,128)}, f32[512,512]{1,0:T(8,128)}, u32[]{:S(2)}, u32[]{:S(2)}) collective-permute-start(f32[512,512]{1,0:T(8,128)} %copy.71), channel_id=1, source_target_pairs={{4,0},{8,4},{12,8},{16,12},{20,16},{24,20},{28,24},{5,1},{9,5},{13... | collective-permute-start | bytes 3145736 | tf_op jit(solution)/shard_map/ppermute | solution.py:15
  316.3 27.3 %copy-start.5 = (f32[512,8,64]{0,2,1:T(8,128)S(1)}, f32[512,8,64]{0,2,1:T(8,128)}, u32[]{:S(2)}) copy-start(f32[512,8,64]{0,2,1:T(8,128)} %copy-done.4) | copy-start | bytes 3145732
  316.3 28.9 %copy-start.15 = (bf16[512,8,32]{0,2,1:T(8,128)(2,1)S(1)}, bf16[512,8,32]{0,2,1:T(8,128)(2,1)}, u32[]{:S(2)}) copy-start(bf16[512,8,32]{0,2,1:T(8,128)(2,1)} %slice.201) | copy-start | bytes 786436
  357.5 40.4 %copy-start.24 = (f32[8,1,256]{2,1,0:T(1,128)S(1)}, f32[8,1,256]{2,1,0:T(1,128)}, u32[]{:S(2)}) copy-start(f32[8,1,256]{2,1,0:T(1,128)} %convert_element_type.155) | copy-start | bytes 24580
  357.5 156.8 %reduce-scatter.12.cloned.1.call-start = ((), (), s32[]{:S(2)}) async-start(), calls=%async_computation.13 | async-start | bytes 5242880 | tf_op jit(solution)/shard_map/reduce_scatter | solution.py:273
  398.0 12.3 %copy-start.33 = (bf16[2048,2048]{1,0:T(8,128)(2,1)S(1)}, bf16[2048,2048]{1,0:T(8,128)(2,1)}, u32[]{:S(2)}) copy-start(bf16[2048,2048]{1,0:T(8,128)(2,1)} %all-gather.14.cloned.1.call-done) | copy-start | bytes 25165828
  410.2 4.8 copy-start.38
  410.2 4.8 copy-start.8
  423.0 170.9 %reduce-scatter.10.cloned.1.call-start = ((), (), s32[]{:S(2)}) async-start(), calls=%async_computation.12 | async-start | bytes 5242880 | tf_op jit(solution)/shard_map/reduce_scatter | solution.py:189
  423.7 11.6 %copy-start.39 = (f32[512,2048]{1,0:T(8,128)S(1)}, f32[512,2048]{1,0:T(8,128)}, u32[]{:S(2)}) copy-start(f32[512,2048]{1,0:T(8,128)} %fusion.76) | copy-start | bytes 12582916
  435.3 8.1 copy-start.13
  446.8 244.5 %reduce-scatter.14.cloned.1.call-start = ((), (), s32[]{:S(2)}) async-start(), calls=%async_computation.14 | async-start | bytes 14155776 | tf_op jit(solution)/shard_map/reduce_scatter | solution.py:278
  455.9 290.9 %reduce-scatter.16.cloned.1.call-start = ((), (), s32[]{:S(2)}) async-start(), calls=%async_computation.15 | async-start | bytes 4718592 | tf_op jit(solution)/shard_map/reduce_scatter | solution.py:280
  460.9 406.1 %reduce-scatter.20.cloned.1.call-start = ((), (), s32[]{:S(2)}) async-start(), calls=%async_computation.17 | async-start | bytes 18874368 | tf_op jit(solution)/shard_map/reduce_scatter | solution.py:283
  475.2 511.8 %reduce-scatter.18.cloned.1.call-start = ((), (), s32[]{:S(2)}) async-start(), calls=%async_computation.16 | async-start | bytes 18874368 | tf_op jit(solution)/shard_map/reduce_scatter | solution.py:281
  486.6 27.7 %copy-start.1 = (bf16[128,2048]{1,0:T(8,128)(2,1)S(1)}, bf16[128,2048]{1,0:T(8,128)(2,1)}, u32[]{:S(2)}) copy-start(bf16[128,2048]{1,0:T(8,128)(2,1)} %param.15) | copy-start | bytes 1572868
  486.6 27.7 %copy-start.17 = (f32[2048]{0:T(1024)S(1)}, f32[2048]{0:T(1024)}, u32[]{:S(2)}) copy-start(f32[2048]{0:T(1024)} %copy-done.16) | copy-start | bytes 24580
  486.6 27.7 %copy-start.23 = (f32[128]{0:T(128)S(1)}, f32[128]{0:T(128)}, u32[]{:S(2)}) copy-start(f32[128]{0:T(128)} %copy-done.22) | copy-start | bytes 1540
  486.6 29.3 %copy-start.32 = (f32[128]{0:T(128)S(1)}, f32[128]{0:T(128)}, u32[]{:S(2)}) copy-start(f32[128]{0:T(128)} %copy-done.31) | copy-start | bytes 1540
  486.6 29.3 %copy-start.26 = (f32[128]{0:T(128)S(1)}, f32[128]{0:T(128)}, u32[]{:S(2)}) copy-start(f32[128]{0:T(128)} %copy-done.25) | copy-start | bytes 1540
  486.6 107.2 %copy-start.3 = (bf16[128,2048]{1,0:T(8,128)(2,1)S(1)}, bf16[128,2048]{1,0:T(8,128)(2,1)}, u32[]{:S(2)}) copy-start(bf16[128,2048]{1,0:T(8,128)(2,1)} %param.26) | copy-start | bytes 1572868
  638.4 349.2 %copy-start.37 = (f32[64]{0:T(128)}, f32[64]{0:T(128)S(1)}, u32[]{:S(2)}) copy-start(f32[64]{0:T(128)S(1)} %dynamic-slice.2) | copy-start | bytes 772
  (15 other events, 29.9 us)
Sparse Core Ops, SparseCore 0:
  58.0 64.5 all-gather.7
  125.0 45.3 all-gather.9
  172.3 33.7 all-gather.11
  207.9 64.8 all-gather.13
  274.6 123.3 all-gather.15
  401.4 33.6 reduce-scatter.21
  437.5 76.7 reduce-scatter.11
  516.6 77.2 reduce-scatter.9
  597.8 93.5 reduce-scatter.13
  695.5 51.3 reduce-scatter.15
  751.0 115.9 reduce-scatter.19
  871.0 115.9 reduce-scatter.17
